TPU v7x, 256 devices: a whole 4x4x8 slice. The times are simulated.
256 devices in a mesh: tp: 2 (over core), row: 16 (over y, x), col: 8 (over z).
Axes of the slice: x: 4, y: 4, z: 8, core: 2. Of those that a mesh axis runs over, the one named last changes fastest.
Arguments:
- acts: bfloat16 [1024, 128, 4096], P(('row', 'col'), None, 'tp'), may hold values from -6 to 6
- grads: bfloat16 [1024, 128, 4096], P(('row', 'col'), None, 'tp'), may hold values from -6 to 6
- proj_in: bfloat16 [4096, 192], P('tp'), may hold values from -0.09375 to 0.09375
- proj_out: bfloat16 [4096, 64], P('tp'), may hold values from -0.09375 to 0.09375
- curvature: float32 [12288, 12288], P('row', ('tp', 'col')), may hold values from -1 to 7, as said below
Outputs:
- trailing: float32 [12288, 12288], P('row', ('tp', 'col'))
- panel: float32 [12288, 512], P('row', 'tp')
Inputs may be any that keep to these rules, and one draw needn't show every extreme that they name: curvature is symmetric.
All inputs are finite; a program needn't handle non-finite values.
Results may differ from a plain program's by a relative error of at most 0.0021.
Values may be sent and summed in bfloat16 or wider, within the bound.
No kernel may reach another device: no remote copies, remote signals or barrier semaphores. Data moves between devices by JAX's collectives and lax.ppermute only.
A program may use at most 64 MiB of HBM per device.

v0:
```python
import jax
import jax.numpy as jnp
from jax import lax
from jax.sharding import PartitionSpec as P

PANEL = 512
precise = lax.Precision.HIGHEST


def spread(block, axis, source):
    block = jnp.where(lax.axis_index(axis) == source, block, jnp.zeros_like(block))
    return lax.psum(block, axis)


def per_device(acts, grads, proj_in, proj_out, curvature):
    tp_count = lax.axis_size("tp")
    row_count = lax.axis_size("row")
    col_count = lax.axis_size("col")
    tp_index = lax.axis_index("tp")
    col_index = lax.axis_index("col")
    ex_dev, seq_len, width = acts.shape
    rows_blk, cols_blk = curvature.shape
    act_width = proj_in.shape[1]
    grad_width = proj_out.shape[1]
    examples = ex_dev * row_count * col_count
    scale = (seq_len * examples) ** (-0.5)
    act_part = jnp.dot(
        acts.reshape(-1, width), proj_in, preferred_element_type=jnp.float32
    ).reshape(ex_dev, seq_len, act_width)
    grad_part = jnp.dot(
        grads.reshape(-1, width), proj_out, preferred_element_type=jnp.float32
    ).reshape(ex_dev, seq_len, grad_width)
    proj_acts, proj_grads = lax.psum((act_part, grad_part), "tp")
    col_width = act_width // (tp_count * col_count)
    act_cols = lax.dynamic_index_in_dim(
        proj_acts.reshape(ex_dev, seq_len, tp_count, col_count, col_width),
        tp_index,
        2,
        keepdims=False,
    )
    col_local = (
        jnp.einsum("escw,esj->cewj", act_cols, proj_grads, precision=precise) * scale
    ).astype(jnp.bfloat16)
    col_local = col_local.reshape(col_count, ex_dev, cols_blk)
    col_mine = lax.all_to_all(col_local, "col", split_axis=0, concat_axis=0, tiled=True)
    row_width = act_width // row_count
    act_rows = proj_acts.reshape(ex_dev, seq_len, row_count, row_width)
    row_local = (
        jnp.einsum("esri,esj->reij", act_rows, proj_grads, precision=precise) * scale
    ).astype(jnp.bfloat16)
    row_local = row_local.reshape(row_count, ex_dev, rows_blk)
    row_mine = lax.all_to_all(row_local, "row", split_axis=0, concat_axis=0, tiled=True)
    row_feats = lax.all_gather(row_mine[None], "col", axis=0, tiled=True)
    folded = lax.dot_general(
        row_feats,
        lax.all_gather(col_mine[:, None], "row", axis=1, tiled=True),
        (((0, 1, 2), (0, 1, 2)), ((), ())),
        preferred_element_type=jnp.float32,
    )
    updated = curvature + folded
    panel_w = PANEL
    block_index = tp_index * col_count + col_index
    owners = -(-panel_w // cols_blk)
    contrib = jnp.where(block_index < owners, updated, jnp.zeros_like(updated))
    panel_cols = lax.psum(contrib[:, :panel_w], ("tp", "col"))
    top_block, diag_block = (
        spread(updated[:panel_w], "row", 0),
        spread(panel_cols[:panel_w], "row", 0),
    )
    diag_factor = jnp.linalg.cholesky(diag_block)
    panel_rows = jax.scipy.linalg.solve_triangular(diag_factor, panel_cols.T, lower=True).T
    top_factor = jax.scipy.linalg.solve_triangular(diag_factor, top_block, lower=True)
    trailing = updated - jnp.dot(
        panel_rows, top_factor, precision=precise, preferred_element_type=jnp.float32
    )
    width_out = panel_w // tp_count
    panel = lax.dynamic_slice_in_dim(panel_rows, tp_index * width_out, width_out, 1)
    return (trailing, panel)


def solution(mesh):
    in_specs = (
        P(("row", "col"), None, "tp"),
        P(("row", "col"), None, "tp"),
        P("tp", None),
        P("tp", None),
        P("row", ("tp", "col")),
    )
    out_specs = (P("row", ("tp", "col")), P("row", "tp"))
    return jax.shard_map(
        per_device, mesh=mesh, in_specs=in_specs, out_specs=out_specs, check_vma=False
    )
```

profile of v0, /device:TPU:1, one launch (start us, length us, event | category | flops | bytes accessed | tf_op | source)
XLA Modules:
  0.0 574.7 jit_solution(4368216738989673927)
XLA Ops:
  8.3 4.7 fusion.29
  13.1 2.1 fusion.41
  15.2 34.9 %all-reduce.11.cloned.1.call-done = (f32[8,128,192]{1,2,0:T(8,128)}, f32[8,128,64]{1,2,0:T(8,128)}) async-done(((f32[8,128,192]{1,2,0:T(8,128)}, f32[8,128,64]{1,2,0:T(8,128)}), (f32[8,128,192]{1,2,0:T(8,128)}, f32[8,128,64]{1,2,0:T(8,128)})) %all-reduce.11.cloned.1.call-update) | async-done | bytes 1048592 | tf_op jit(solution)/shard_map/psum | solution.py:33
  53.4 13.7 %all_to_all.10 = bf16[16,8,768]{2,1,0:T(8,128)(2,1)} all-to-all(bf16[16,8,768]{2,1,0:T(8,128)(2,1)S(1)} %reshape.60), channel_id=1, replica_groups=mesh['tp'=2,'row'=16,'col'=8] {'row'}, dimensions={0} | all-to-all | bytes 393216 | tf_op jit(solution)/shard_map/all_to_all | solution.py:52
  68.1 14.3 %all_to_all.11 = bf16[8,8,768]{2,1,0:T(8,128)(2,1)} all-to-all(bf16[8,8,768]{2,1,0:T(8,128)(2,1)S(1)} %copy.78), channel_id=1, replica_groups=mesh['tp'=2,'row'=16,'col'=8] {'col'}, dimensions={0} | all-to-all | bytes 196608 | tf_op jit(solution)/shard_map/all_to_all | solution.py:45
  82.5 3.1 copy.52
  85.5 16.1 %all-gather.5.cloned.1.call-done = bf16[128,8,768]{2,1,0:T(8,128)(2,1)} async-done(((bf16[16,8,768]{2,1,0:T(8,128)(2,1)}), bf16[128,8,768]{2,1,0:T(8,128)(2,1)}) %all-gather.5.cloned.1.call-update) | async-done | bytes 1572880 | tf_op jit(solution)/shard_map/all_gather | solution.py:53
  101.7 51.3 %all-gather.7.cloned.1.call-done = bf16[8,128,768]{2,1,0:T(8,128)(2,1)} async-done(((bf16[8,8,768]{2,1,0:T(8,128)(2,1)}), bf16[8,128,768]{2,1,0:T(8,128)(2,1)}) %all-gather.7.cloned.1.call-update) | async-done | bytes 1572880 | tf_op jit(solution)/shard_map/all_gather | solution.py:56
  153.0 4.1 bitcast_add_fusion
  159.9 114.0 %all-reduce.7.cloned.1.call-done = f32[768,512]{0,1:T(8,128)} async-done(((f32[768,512]{0,1:T(8,128)}), f32[768,512]{0,1:T(8,128)}) %all-reduce.7.cloned.1.call-update) | async-done | bytes 1572880 | tf_op jit(solution)/shard_map/psum | solution.py:65
  273.9 2.3 slice_select_fusion.2
  276.2 104.4 %all-reduce.9.cloned.1.call-done = (f32[512,768]{0,1:T(8,128)}, f32[512,512]{0,1:T(8,128)}) async-done(((f32[512,768]{0,1:T(8,128)}, f32[512,512]{0,1:T(8,128)}), (f32[512,768]{0,1:T(8,128)}, f32[512,512]{0,1:T(8,128)})) %all-reduce.9.cloned.1.call-update) | async-done | bytes 2621456 | tf_op jit(solution)/shard_map/psum | solution.py:12
  380.6 2.5 copy.54
  383.1 1.8 fusion.22
  385.9 11.7 %cholesky.103 = f32[128,128]{1,0:T(8,128)S(1)} custom-call(f32[128,128]{1,0:T(8,128)S(1)} %cholesky.263), custom_call_target="Cholesky" | custom-call | tf_op jit(solution)/shard_map/jit(cholesky)/cholesky | solution.py:70
  398.4 9.8 %custom-call.30 = f32[1,128,128]{1,2,0:T(8,128)S(1)} custom-call(f32[1,128,128]{2,1,0:T(8,128)S(1)} %get-tuple-element.68), custom_call_target="InvertDiagBlocksLowerTriangular" | custom-call | tf_op jit(solution)/shard_map/jit(cholesky)/cholesky | solution.py:70
  412.1 13.2 %cholesky.215 = f32[128,128]{1,0:T(8,128)} custom-call(f32[128,128]{1,0:T(8,128)} %cholesky.267), custom_call_target="Cholesky" | custom-call | tf_op jit(solution)/shard_map/jit(cholesky)/cholesky | solution.py:70
  428.3 11.6 %custom-call.31 = f32[1,128,128]{1,2,0:T(8,128)} custom-call(f32[1,128,128]{2,1,0:T(8,128)} %get-tuple-element.66), custom_call_target="InvertDiagBlocksLowerTriangular" | custom-call | tf_op jit(solution)/shard_map/jit(cholesky)/cholesky | solution.py:70
  444.7 11.7 %cholesky.236 = f32[128,128]{1,0:T(8,128)S(1)} custom-call(f32[128,128]{1,0:T(8,128)S(1)} %cholesky.272), custom_call_target="Cholesky" | custom-call | tf_op jit(solution)/shard_map/jit(cholesky)/cholesky | solution.py:70
  457.2 9.8 %custom-call.32 = f32[1,128,128]{1,2,0:T(8,128)S(1)} custom-call(f32[1,128,128]{2,1,0:T(8,128)S(1)} %get-tuple-element.64), custom_call_target="InvertDiagBlocksLowerTriangular" | custom-call | tf_op jit(solution)/shard_map/jit(cholesky)/cholesky | solution.py:70
  469.4 11.9 %cholesky.253 = f32[128,128]{1,0:T(8,128)S(1)} custom-call(f32[128,128]{1,0:T(8,128)S(1)} %convolution_subtract_fusion.9), custom_call_target="Cholesky" | custom-call | tf_op jit(solution)/shard_map/jit(cholesky)/cholesky | solution.py:70
  486.5 2.3 select_select_fusion
  488.9 14.5 %while.4 = (s32[]{:T(128)}, f32[512,512]{0,1:T(8,128)}, s32[4,2]{0,1:T(2,128)S(1)}, f32[4,128,128]{2,1,0:T(8,128)}, s32[]{:T(128)}) while((s32[]{:T(128)}, f32[512,512]{0,1:T(8,128)}, s32[4,2]{0,1:T(2,128)S(1)}, f32[4,128,128]{2,1,0:T(8,128)}, s32[]{:T(128)}) %tuple.41), condition=%wide.while_cond, body=%wide.while_body.sunk | while | flops 2 | bytes 393329 | solution.py:71
  489.5 2.2 dynamic-slice.14
  493.2 2.2 dynamic-slice.14
  496.8 2.2 dynamic-slice.14
  500.5 2.2 dynamic-slice.14
  503.4 40.1 %custom-call.34 = f32[4,128,128]{1,2,0:T(8,128)S(1)} custom-call(f32[4,128,128]{2,1,0:T(8,128)} %get-tuple-element.17), custom_call_target="InvertDiagBlocksLowerTriangular" | custom-call | tf_op jit(solution)/shard_map/jit(_solve_triangular)/triangular_solve | solution.py:71
  545.2 1.8 convolution_subtract_fusion.2
  549.5 2.1 convolution_subtract_fusion.1
  557.6 6.1 %convolution_subtract_fusion = f32[768,768]{0,1:T(8,128)} fusion(f32[768,768]{0,1:T(8,128)S(1)} %bitcast_add_fusion, f32[128,768]{1,0:T(8,128)S(1)} %fusion.61, f32[128,768]{1,0:T(8,128)S(1)} %fusion.59, f32[128,768]{1,0:T(8,128)S(1)} %fusion.57, f32[128,768]{1,0:T(8,128)S(1)} %fusion.34, f32[128,768]{1,0:T(8,128)S(1)} %fusion.62, ...), kind=kOutput, calls=%fused_computation.3 | convolution fusion | flops 3626827776 | bytes 7864320 | tf_op jit(solution)/shard_map/dot_general | solution.py:73
  563.6 3.2 copy.68
  (106 shorter events, 44.3 us)
Async XLA Ops:
  7.2 1.1 copy-start
  7.2 5.9 %copy-start.11 = (bf16[2048,64]{0,1:T(8,128)(2,1)S(1)}, bf16[2048,64]{0,1:T(8,128)(2,1)}, u32[]{:S(2)}) copy-start(bf16[2048,64]{0,1:T(8,128)(2,1)} %param.10) | copy-start | bytes 786436
  7.2 43.0 %all-reduce.11.cloned.1.call-start = ((), (), s32[]{:S(2)}) async-start(), calls=%async_computation.6 | async-start | bytes 2097152 | tf_op jit(solution)/shard_map/psum | solution.py:33
  8.3 4.8 copy-start.4
  15.2 86.5 %all-gather.5.cloned.1.call-start = ((), (), s32[]{:S(2)}) async-start(), calls=%async_computation.3 | async-start | bytes 1769472 | tf_op jit(solution)/shard_map/all_gather | solution.py:53
  50.2 1.6 copy-start.8
  67.2 85.8 %all-gather.7.cloned.1.call-start = ((), (), s32[]{:S(2)}) async-start(), calls=%async_computation.4 | async-start | bytes 1671168 | tf_op jit(solution)/shard_map/all_gather | solution.py:56
  82.4 191.5 %all-reduce.7.cloned.1.call-start = ((), (), s32[]{:S(2)}) async-start(), calls=%async_computation.2 | async-start | bytes 3145728 | tf_op jit(solution)/shard_map/psum | solution.py:65
  158.3 222.3 %all-reduce.9.cloned.1.call-start = ((), (), s32[]{:S(2)}) async-start(), calls=%async_computation.5 | async-start | bytes 5242880 | tf_op jit(solution)/shard_map/psum | solution.py:12
  384.9 1.0 copy-start.6
  410.8 0.7 copy-start.9
  412.1 29.7 %copy-start.10 = (f32[384,128]{1,0:T(8,128)S(1)}, f32[384,128]{1,0:T(8,128)}, u32[]{:S(2)}) copy-start(f32[384,128]{1,0:T(8,128)} %copy-done.9) | copy-start | bytes 589828
  440.0 1.9 copy-start.12
  442.2 1.0 copy-start.1
  543.5 4.1 copy-start.2
  543.5 4.1 copy-start.7
  549.5 2.7 copy-start.3
  563.6 3.2 copy-start.5
Sparse Core Ops, SparseCore 0:
  15.3 34.7 all-reduce.10
  67.3 34.3 all-gather.4
  104.2 48.7 all-gather.6
  158.5 115.3 all-reduce.6
  277.7 102.8 all-reduce.8
where the time goes:
time: 581 us; the launch traced here: 575 us
  waiting for transfers between devices  321 us (55%)
  other arithmetic  134 us (23%)
  matrix products  38.2 us (7%)
  local copies, waits for them, and re-layouts  36.7 us (6%)
  blocking collectives  28.1 us (5%)
  between operations  16.9 us (3%)
    psum x1, waiting for transfers between devices, per_device(): panel_cols = lax.psum(contrib[:, :panel_w], ('tp', 'col'))  114 us
    psum x1, waiting for transfers between devices, spread(): return lax.psum(block, axis)  104 us
    another operation x14, other arithmetic, per_device(): diag_factor = jnp.linalg.cholesky(diag_block)  83.3 us
    all_gather x1, waiting for transfers between devices, per_device(): lax.all_gather(col_mine[:, None], 'row', axis=1, tiled=True)  51.3 us
    another operation x5, other arithmetic, per_device(): jax.scipy.linalg.solve_triangular(diag_factor, panel_cols.T, lower=True)  43.7 us
    psum x1, waiting for transfers between devices, per_device(): proj_acts, proj_grads = lax.psum((act_part, grad_part), 'tp')  34.9 us
    all_gather x1, waiting for transfers between devices, per_device(): row_feats = lax.all_gather(row_mine[None], 'col', axis=0, tiled=True)  16.1 us
    another operation x21, local copies, waits for them, and re-layouts, per_device(): jax.scipy.linalg.solve_triangular(diag_factor, panel_cols.T, lower=True)  14.4 us
  transfers between devices with their start and end apart: 5, of which 5 were waited for; matrix products, arithmetic and copies ran while one was open for 1% of the time, Pallas kernels for 0%

commit v1 on v0

--- a/solution.py
+++ b/solution.py
@@ -53,7 +53,10 @@
     row_feats = lax.all_gather(row_mine[None], "col", axis=0, tiled=True)
     folded = lax.dot_general(
         row_feats,
-        lax.all_gather(col_mine[:, None], "row", axis=1, tiled=True),
+        jnp.concatenate(
+            lax.all_to_all(jnp.stack([col_mine[:, None]] * lax.axis_size("row")), "row", 0, 0),
+            axis=1,
+        ),
         (((0, 1, 2), (0, 1, 2)), ((), ())),
         preferred_element_type=jnp.float32,
     )

time: 581 us -> 531 us (0.914)
  waiting for transfers between devices: 321 us -> 266 us
    all_gather x1 -> x0, waiting for transfers between devices: 51.3 us -> none  [per_device(): lax.all_gather(col_mine[:, None], 'row', axis=1, tiled=True)]
    all_to_all x0 -> x1, waiting for transfers between devices: none -> 17.6 us  [per_device(): lax.all_to_all(jnp.stack([col_mine[:, None]] * lax.axis_size('row')), 'ro...]
    all_gather x1, waiting for transfers between devices: 16.1 us -> 0.01 us  [per_device(): row_feats = lax.all_gather(row_mine[None], 'col', axis=0, tiled=True)]
  transfers between devices with their start and end apart: 5 -> 5, of which waited for: 5 -> 4; matrix products, arithmetic and copies ran while one was open for 1% -> 1% of each run, Pallas kernels for 0% -> 0%
where the time goes in v1:
time: 531 us; the launch traced here: 524 us
  waiting for transfers between devices  266 us (50%)
  other arithmetic  134 us (25%)
  matrix products  38.1 us (7%)
  local copies, waits for them, and re-layouts  37 us (7%)
  blocking collectives  27.9 us (5%)
  between operations  16.9 us (3%)
    psum x1, waiting for transfers between devices, per_device(): panel_cols = lax.psum(contrib[:, :panel_w], ('tp', 'col'))  109 us
    psum x1, waiting for transfers between devices, spread(): return lax.psum(block, axis)  104 us
    another operation x14, other arithmetic, per_device(): diag_factor = jnp.linalg.cholesky(diag_block)  83.3 us
    another operation x5, other arithmetic, per_device(): jax.scipy.linalg.solve_triangular(diag_factor, panel_cols.T, lower=True)  43.7 us
    psum x1, waiting for transfers between devices, per_device(): proj_acts, proj_grads = lax.psum((act_part, grad_part), 'tp')  34.9 us
    all_to_all x1, waiting for transfers between devices, per_device(): lax.all_to_all(jnp.stack([col_mine[:, None]] * lax.axis_size('row')), 'ro...  17.6 us
    another operation x21, local copies, waits for them, and re-layouts, per_device(): jax.scipy.linalg.solve_triangular(diag_factor, panel_cols.T, lower=True)  14.4 us
    all_to_all x1, blocking collectives, per_device(): lax.all_to_all(col_local, 'col', split_axis=0, concat_axis=0, tiled=True)  14.2 us
  transfers between devices with their start and end apart: 5, of which 4 were waited for; matrix products, arithmetic and copies ran while one was open for 1% of the time, Pallas kernels for 0%

profile of v1, /device:TPU:1, one launch (start us, length us, event | category | flops | bytes accessed | tf_op | source)
XLA Modules:
  0.0 524.4 jit_solution(5895107987484112983)
XLA Ops:
  8.3 4.7 fusion.30
  13.1 2.1 fusion.42
  15.2 34.9 %all-reduce.11.cloned.1.call-done = (f32[8,128,192]{1,2,0:T(8,128)}, f32[8,128,64]{1,2,0:T(8,128)}) async-done(((f32[8,128,192]{1,2,0:T(8,128)}, f32[8,128,64]{1,2,0:T(8,128)}), (f32[8,128,192]{1,2,0:T(8,128)}, f32[8,128,64]{1,2,0:T(8,128)})) %all-reduce.11.cloned.1.call-update) | async-done | bytes 1048592 | tf_op jit(solution)/shard_map/psum | solution.py:33
  53.4 13.7 %all_to_all.15 = bf16[16,8,768]{2,1,0:T(8,128)(2,1)} all-to-all(bf16[16,8,768]{2,1,0:T(8,128)(2,1)S(1)} %reshape.68), channel_id=1, replica_groups=mesh['tp'=2,'row'=16,'col'=8] {'row'}, dimensions={0} | all-to-all | bytes 393216 | tf_op jit(solution)/shard_map/all_to_all | solution.py:52
  68.0 14.2 %all_to_all.16 = bf16[8,8,768]{2,1,0:T(8,128)(2,1)S(1)} all-to-all(bf16[8,8,768]{2,1,0:T(8,128)(2,1)S(1)} %copy.79), channel_id=1, replica_groups=mesh['tp'=2,'row'=16,'col'=8] {'col'}, dimensions={0} | all-to-all | bytes 196608 | tf_op jit(solution)/shard_map/all_to_all | solution.py:45
  83.6 4.5 all-to-all-start.2
  88.2 2.0 copy.53
  90.1 17.6 %all-to-all-done.2 = bf16[16,8,1,8,768]{4,3,1,2,0:T(8,128)(2,1)} async-done(((bf16[16,8,1,8,768]{4,3,1,2,0:T(8,128)(2,1)}), bf16[16,8,1,8,768]{4,3,1,2,0:T(8,128)(2,1)}, u32[]{:S(2)}, u32[]{:S(2)}) %all-to-all-start.2) | async-done | bytes 1572896 | tf_op jit(solution)/shard_map/all_to_all | solution.py:57
  107.7 4.0 bitcast_add_fusion
  114.7 108.9 %all-reduce.7.cloned.1.call-done = f32[768,512]{0,1:T(8,128)} async-done(((f32[768,512]{0,1:T(8,128)}), f32[768,512]{0,1:T(8,128)}) %all-reduce.7.cloned.1.call-update) | async-done | bytes 1572880 | tf_op jit(solution)/shard_map/psum | solution.py:68
  223.5 2.3 slice_select_fusion.2
  225.9 104.4 %all-reduce.9.cloned.1.call-done = (f32[512,768]{0,1:T(8,128)}, f32[512,512]{0,1:T(8,128)}) async-done(((f32[512,768]{0,1:T(8,128)}, f32[512,512]{0,1:T(8,128)}), (f32[512,768]{0,1:T(8,128)}, f32[512,512]{0,1:T(8,128)})) %all-reduce.9.cloned.1.call-update) | async-done | bytes 2621456 | tf_op jit(solution)/shard_map/psum | solution.py:12
  330.3 2.5 copy.55
  332.8 1.8 fusion.23
  335.5 11.7 %cholesky.103 = f32[128,128]{1,0:T(8,128)S(1)} custom-call(f32[128,128]{1,0:T(8,128)S(1)} %cholesky.263), custom_call_target="Cholesky" | custom-call | tf_op jit(solution)/shard_map/jit(cholesky)/cholesky | solution.py:73
  348.0 9.8 %custom-call.30 = f32[1,128,128]{1,2,0:T(8,128)S(1)} custom-call(f32[1,128,128]{2,1,0:T(8,128)S(1)} %get-tuple-element.68), custom_call_target="InvertDiagBlocksLowerTriangular" | custom-call | tf_op jit(solution)/shard_map/jit(cholesky)/cholesky | solution.py:73
  361.8 13.2 %cholesky.215 = f32[128,128]{1,0:T(8,128)} custom-call(f32[128,128]{1,0:T(8,128)} %cholesky.267), custom_call_target="Cholesky" | custom-call | tf_op jit(solution)/shard_map/jit(cholesky)/cholesky | solution.py:73
  378.0 11.6 %custom-call.31 = f32[1,128,128]{1,2,0:T(8,128)} custom-call(f32[1,128,128]{2,1,0:T(8,128)} %get-tuple-element.66), custom_call_target="InvertDiagBlocksLowerTriangular" | custom-call | tf_op jit(solution)/shard_map/jit(cholesky)/cholesky | solution.py:73
  394.3 11.7 %cholesky.236 = f32[128,128]{1,0:T(8,128)S(1)} custom-call(f32[128,128]{1,0:T(8,128)S(1)} %cholesky.272), custom_call_target="Cholesky" | custom-call | tf_op jit(solution)/shard_map/jit(cholesky)/cholesky | solution.py:73
  406.8 9.8 %custom-call.32 = f32[1,128,128]{1,2,0:T(8,128)S(1)} custom-call(f32[1,128,128]{2,1,0:T(8,128)S(1)} %get-tuple-element.64), custom_call_target="InvertDiagBlocksLowerTriangular" | custom-call | tf_op jit(solution)/shard_map/jit(cholesky)/cholesky | solution.py:73
  419.1 11.9 %cholesky.253 = f32[128,128]{1,0:T(8,128)S(1)} custom-call(f32[128,128]{1,0:T(8,128)S(1)} %convolution_subtract_fusion.9), custom_call_target="Cholesky" | custom-call | tf_op jit(solution)/shard_map/jit(cholesky)/cholesky | solution.py:73
  436.2 2.3 select_select_fusion
  438.5 14.5 %while.4 = (s32[]{:T(128)}, f32[512,512]{0,1:T(8,128)}, s32[4,2]{0,1:T(2,128)S(1)}, f32[4,128,128]{2,1,0:T(8,128)}, s32[]{:T(128)}) while((s32[]{:T(128)}, f32[512,512]{0,1:T(8,128)}, s32[4,2]{0,1:T(2,128)S(1)}, f32[4,128,128]{2,1,0:T(8,128)}, s32[]{:T(128)}) %tuple.41), condition=%wide.while_cond, body=%wide.while_body.sunk | while | flops 2 | bytes 393329 | solution.py:74
  439.2 2.2 dynamic-slice.14
  442.8 2.2 dynamic-slice.14
  446.5 2.2 dynamic-slice.14
  450.1 2.2 dynamic-slice.14
  453.0 40.1 %custom-call.34 = f32[4,128,128]{1,2,0:T(8,128)S(1)} custom-call(f32[4,128,128]{2,1,0:T(8,128)} %get-tuple-element.17), custom_call_target="InvertDiagBlocksLowerTriangular" | custom-call | tf_op jit(solution)/shard_map/jit(_solve_triangular)/triangular_solve | solution.py:74
  494.8 1.8 convolution_subtract_fusion.2
  499.2 2.1 convolution_subtract_fusion.1
  507.2 6.1 %convolution_subtract_fusion = f32[768,768]{0,1:T(8,128)} fusion(f32[768,768]{0,1:T(8,128)S(1)} %bitcast_add_fusion, f32[128,768]{1,0:T(8,128)S(1)} %fusion.62, f32[128,768]{1,0:T(8,128)S(1)} %fusion.60, f32[128,768]{1,0:T(8,128)S(1)} %fusion.58, f32[128,768]{1,0:T(8,128)S(1)} %fusion.35, f32[128,768]{1,0:T(8,128)S(1)} %fusion.63, ...), kind=kOutput, calls=%fused_computation.3 | convolution fusion | flops 3626827776 | bytes 7864320 | tf_op jit(solution)/shard_map/dot_general | solution.py:76
  513.3 3.2 copy.69
  (108 shorter events, 45.5 us)
Async XLA Ops:
  7.2 1.1 copy-start
  7.2 5.9 %copy-start.12 = (bf16[2048,64]{0,1:T(8,128)(2,1)S(1)}, bf16[2048,64]{0,1:T(8,128)(2,1)}, u32[]{:S(2)}) copy-start(bf16[2048,64]{0,1:T(8,128)(2,1)} %param.10) | copy-start | bytes 786436
  7.2 43.0 %all-reduce.11.cloned.1.call-start = ((), (), s32[]{:S(2)}) async-start(), calls=%async_computation.6 | async-start | bytes 2097152 | tf_op jit(solution)/shard_map/psum | solution.py:33
  8.3 4.8 copy-start.4
  15.2 92.5 %all-gather.3.cloned.1.call-start = ((), (), s32[]{:S(2)}) async-start(), calls=%async_computation.4 | async-start | bytes 1769472 | tf_op jit(solution)/shard_map/all_gather | solution.py:53
  50.2 1.6 copy-start.9
  83.6 4.6 copy-start.7
  83.6 24.1 %all-to-all-start.2 = ((bf16[16,8,1,8,768]{4,3,1,2,0:T(8,128)(2,1)}), bf16[16,8,1,8,768]{4,3,1,2,0:T(8,128)(2,1)}, u32[]{:S(2)}, u32[]{:S(2)}) async-start(bf16[16,8,1,8,768]{4,3,1,2,0:T(8,128)(2,1)} %stack.3), calls=%async_computation.2 | async-start | bytes 3145728 | tf_op jit(solution)/shard_map/all_to_all | solution.py:57
  88.1 135.4 %all-reduce.7.cloned.1.call-start = ((), (), s32[]{:S(2)}) async-start(), calls=%async_computation.3 | async-start | bytes 3145728 | tf_op jit(solution)/shard_map/psum | solution.py:68
  113.1 217.2 %all-reduce.9.cloned.1.call-start = ((), (), s32[]{:S(2)}) async-start(), calls=%async_computation.5 | async-start | bytes 5242880 | tf_op jit(solution)/shard_map/psum | solution.py:12
  334.6 1.0 copy-start.6
  360.5 0.7 copy-start.10
  361.8 29.7 %copy-start.11 = (f32[384,128]{1,0:T(8,128)S(1)}, f32[384,128]{1,0:T(8,128)}, u32[]{:S(2)}) copy-start(f32[384,128]{1,0:T(8,128)} %copy-done.10) | copy-start | bytes 589828
  389.6 1.9 copy-start.13
  391.8 1.0 copy-start.1
  493.1 4.1 copy-start.2
  493.2 4.1 copy-start.8
  499.2 2.7 copy-start.3
  513.3 3.2 copy-start.5
Sparse Core Ops, SparseCore 0:
  15.3 34.7 all-reduce.10
  67.3 34.5 all-gather.2
  113.2 110.3 all-reduce.6
  227.4 102.8 all-reduce.8
